TPU v7x, 32 devices: a whole 2x2x4 slice. The times are simulated.
32 devices in a mesh: gx: 4 (over z), gy: 4 (over y, core), col: 2 (over x).
Axes of the slice: x: 2, y: 2, z: 4, core: 2. Of those that a mesh axis runs over, the one named last changes fastest.
Arguments:
- sources: float32 [4, 4, 2, 128, 1152], P('gx', 'gy', None, 'col'), may hold values from -100 to 100
- impedance: bfloat16 [4, 4, 2, 1152, 1152], P('gx', 'gy'), may hold values from -0.09375 to 0.09375
- pair_maps: bfloat16 [4, 4, 2, 2, 384, 384], P('gx', 'gy'), may hold values from -0.21875 to 0.21875
- lead_side: int32 [4, 4, 2], P('gx', 'gy'), may hold values from 0 to 1
- coarse_basis: float32 [4, 4, 32, 2, 1152], P('gx', 'gy'), may hold values from -0.125 to 0.125
- coarse_inverse: float32 [512, 512], P(('gx', 'gy', 'col')), may hold values from -0.6 to 0.6
Outputs:
- solution_traces: float32 [4, 4, 2, 128, 1152], P('gx', 'gy', None, 'col')
Inputs may be any that keep to these rules, and one draw needn't show every extreme that they name: `lead_side`: entries of interfaces beyond the last subdomain along a dimension are read by no step.
All inputs are finite; a program needn't handle non-finite values.
Results may differ from a plain program's by a relative error of at most 0.0039.
Values may be sent and summed in bfloat16 or wider, within the bound.
No kernel may reach another device: no remote copies, remote signals or barrier semaphores. Data moves between devices by JAX's collectives and lax.ppermute only.
A program may use at most 64 MiB of HBM per device.

v0:
```python
import jax
import jax.numpy as jnp
from jax import lax
from jax.sharding import PartitionSpec as P

ITERS = 2
STEP_RATIO = 0.4


def shifted(block, axis, distance):
    devices = range(lax.axis_size(axis))
    route = [(i - distance, i) for i in devices if i - distance in devices]
    return lax.ppermute(block, axis, route)


def complex_apply(traces, real_part, imag_part):
    sources_here = traces.shape[1]
    flattened = traces.reshape(2 * sources_here, traces.shape[2])
    first_part = jnp.dot(flattened, real_part, preferred_element_type=jnp.float32).reshape(
        2, sources_here, -1
    )
    second_part = jnp.dot(flattened, imag_part, preferred_element_type=jnp.float32).reshape(
        2, sources_here, -1
    )
    return jnp.stack([first_part[0] - second_part[1], second_part[0] + first_part[1]])


def pair_solve(lower_side, upper_side, solver):
    return complex_apply(jnp.concatenate([lower_side, upper_side], axis=2), solver[0], solver[1])


def orient(solver, leading, face_width):
    swapped = jnp.roll(solver, (face_width, face_width), axis=(1, 2))
    return jnp.where(leading == 0, solver, swapped)


def per_device(sources, impedance, pair_maps, lead_side, coarse_basis, coarse_inverse):
    drive_traces = sources[0, 0]
    sources_here = drive_traces.shape[1]
    face_width = drive_traces.shape[2] // 6
    map_real = impedance[0, 0, 0]
    map_imag = impedance[0, 0, 1]
    basis_here = coarse_basis[0, 0]
    coarse_count = basis_here.shape[0]
    first_count = lax.axis_size("gx")
    second_count = lax.axis_size("gy")
    first_index = lax.axis_index("gx")
    second_index = lax.axis_index("gy")
    first_solver = orient(pair_maps[0, 0, 0], lead_side[0, 0, 0], face_width)
    second_solver = orient(pair_maps[0, 0, 1], lead_side[0, 0, 1], face_width)
    pair_rows = lax.all_gather(coarse_inverse, "col", axis=0, tiled=True)
    row_blocks = pair_rows.reshape(coarse_count, -1, coarse_count)
    iterate = jnp.zeros(drive_traces.shape, jnp.float32)
    for repeat in range(ITERS):
        rounded = iterate.astype(jnp.bfloat16)
        outgoing = (complex_apply(rounded, map_real, map_imag) + drive_traces).astype(jnp.bfloat16)
        first_faces = outgoing[:, :, : 2 * face_width].reshape(2, sources_here, 2, face_width)
        second_faces = outgoing[:, :, 2 * face_width : 4 * face_width].reshape(
            2, sources_here, 2, face_width
        )
        first_above = shifted(first_faces[:, :, 0], "gx", -1)
        second_above = shifted(second_faces[:, :, 0], "gy", -1)
        first_solved = pair_solve(first_faces[:, :, 1], first_above, first_solver)
        second_solved = pair_solve(second_faces[:, :, 1], second_above, second_solver)
        face_one = first_solved[:, :, :face_width]
        face_three = second_solved[:, :, :face_width]
        face_zero = shifted(first_solved[:, :, face_width:], "gx", 1)
        face_two = shifted(second_solved[:, :, face_width:], "gy", 1)
        face_one = jnp.where(first_index < first_count - 1, face_one, 0.0)
        face_three = jnp.where(second_index < second_count - 1, face_three, 0.0)
        updated = jnp.concatenate(
            [
                face_zero,
                face_one,
                face_two,
                face_three,
                outgoing[:, :, 5 * face_width :].astype(jnp.float32),
                outgoing[:, :, 4 * face_width : 5 * face_width].astype(jnp.float32),
            ],
            axis=2,
        )
        defect = updated - iterate
        projected = jnp.einsum("csk,pck->sp", defect, basis_here, precision=lax.Precision.HIGHEST)
        gathered = lax.all_gather(projected[None], ("gx", "gy"), axis=0, tiled=True)
        coarse = jnp.einsum("nsp,qnp->sq", gathered, row_blocks, precision=lax.Precision.HIGHEST)
        correction = jnp.einsum("sp,pck->csk", coarse, basis_here, precision=lax.Precision.HIGHEST)
        defect_norm, correction_norm = lax.psum(
            (jnp.sum(defect * defect, axis=(0, 2)), jnp.sum(correction * correction, axis=(0, 2))),
            ("gx", "gy"),
        )
        factor = STEP_RATIO * jnp.sqrt(defect_norm / (correction_norm + 1e-06))
        iterate = updated + factor[None, :, None] * correction
    return iterate[None, None]


def solution(mesh):
    return jax.shard_map(
        per_device,
        mesh=mesh,
        in_specs=(
            P("gx", "gy", None, "col", None),
            P("gx", "gy", None, None, None),
            P("gx", "gy", None, None, None, None),
            P("gx", "gy", None),
            P("gx", "gy", None, None, None),
            P(("gx", "gy", "col"), None),
        ),
        out_specs=P("gx", "gy", None, "col", None),
        check_vma=False,
    )
```

profile of v0, /device:TPU:0, one launch (start us, length us, event | category | flops | bytes accessed | tf_op | source)
XLA Modules:
  0.0 154.8 jit_solution(12876421462017243072)
XLA Ops:
  0.0 2.4 %fusion.2 = f32[128,1152]{1,0:T(8,128)S(1)} fusion(bf16[1,1,2,1152,1152]{4,3,2,1,0:T(8,128)(2,1)} %param.7), kind=kOutput, calls=%fused_computation.2 | convolution fusion | flops 339738624 | bytes 3244032 | tf_op jit(solution)/shard_map/dot_general | solution.py:22
  2.4 2.4 %fusion.6 = f32[128,1152]{1,0:T(8,128)S(1)} fusion(bf16[1,1,2,1152,1152]{4,3,2,1,0:T(8,128)(2,1)} %param.7), kind=kOutput, calls=%fused_computation.6 | convolution fusion | flops 339738624 | bytes 3244032 | tf_op jit(solution)/shard_map/dot_general | solution.py:19
  5.1 0.8 fusion.79
  6.0 1.3 collective-permute-start.2
  7.4 0.2 fusion.80
  7.6 1.3 collective-permute-start
  9.1 0.6 fusion.81
  11.0 0.2 fusion.20
  11.2 0.2 fusion.19
  11.4 0.6 fusion.13
  12.2 0.3 fusion.32
  12.5 0.3 fusion.30
  12.7 2.4 %collective-permute-done = bf16[2,64,192]{2,1,0:T(8,128)(2,1)S(1)} collective-permute-done((bf16[2,64,192]{2,1,0:T(8,128)(2,1)S(1)}, bf16[2,64,192]{2,1,0:T(8,128)(2,1)S(1)}, u32[]{:S(2)}, u32[]{:S(2)}) %collective-permute-start) | collective-permute-done | bytes 49184 | tf_op jit(solution)/shard_map/ppermute | solution.py:13
  15.1 0.3 fusion.28
  15.4 0.3 fusion.26
  15.8 2.2 %collective-permute-start.3 = (f32[2,64,192]{2,1,0:T(8,128)S(1)}, f32[2,64,192]{2,1,0:T(8,128)S(1)}, u32[]{:S(2)}, u32[]{:S(2)}) collective-permute-start(f32[2,64,192]{2,1,0:T(8,128)S(1)} %get-tuple-element.44), channel_id=1, source_target_pairs={{0,2},{2,4},{4,6},{1,3},{3,5},{5,7},{8,10},{10,12},{12,14},{9,11},... | collective-permute-start | bytes 294920 | tf_op jit(solution)/shard_map/ppermute | solution.py:13
  18.1 4.1 %collective-permute-start.1 = (f32[2,64,192]{2,1,0:T(8,128)S(1)}, f32[2,64,192]{2,1,0:T(8,128)S(1)}, u32[]{:S(2)}, u32[]{:S(2)}) collective-permute-start(f32[2,64,192]{2,1,0:T(8,128)S(1)} %get-tuple-element.46), channel_id=1, source_target_pairs={{0,8},{8,16},{16,24},{1,9},{9,17},{17,25},{2,10},{10,18},{18,26},{... | collective-permute-start | bytes 294920 | tf_op jit(solution)/shard_map/ppermute | solution.py:13
  22.3 4.6 %all_gather.10 = f32[32,512]{1,0:T(8,128)S(1)} all-gather(f32[16,512]{1,0:T(8,128)S(1)} %copy-done.5), channel_id=1, replica_groups=mesh['gx'=4,'gy'=4,'col'=2] {'col'}, dimensions={0}, use_global_device_ids=true | all-gather | bytes 98304 | tf_op jit(solution)/shard_map/all_gather | solution.py:51
  27.0 0.2 concatenate.62
  27.4 0.6 convolution_bitcast_fusion.1
  28.0 21.0 %all-gather.2 = f32[16,64,32]{1,2,0:T(8,128)S(1)} all-gather(f32[1,64,32]{1,2,0:T(8,128)S(1)} %convolution_bitcast_fusion.1), channel_id=2, replica_groups=mesh['gx'=4,'gy'=4,'col'=2] {'gx','gy'}, dimensions={0}, use_global_device_ids=true | all-gather | bytes 139264 | tf_op jit(solution)/shard_map/all_gather | solution.py:84
  49.0 0.5 fusion.36
  49.6 0.8 multiply_reduce_fusion.2
  50.4 29.8 %all-reduce.1 = (f32[64]{0:T(128)S(1)}, f32[64]{0:T(128)S(1)}) all-reduce(f32[64]{0:T(128)S(1)} %multiply_reduce_fusion.3, f32[64]{0:T(128)S(1)} %get-tuple-element.57), channel_id=1, replica_groups=mesh['gx'=4,'gy'=4,'col'=2] {'gx','gy'}, use_global_device_ids=true, to_apply=%region_1.2 | all-reduce | flops 128 | bytes 1024 | tf_op jit(solution)/shard_map/psum | solution.py:87
  80.2 0.1 fusion.72
  80.4 2.3 %fusion = f32[128,1152]{1,0:T(8,128)S(1)} fusion(bf16[128,1152]{1,0:T(8,128)(2,1)S(1)} %bitcast.121, bf16[1,1,2,1152,1152]{4,3,2,1,0:T(8,128)(2,1)} %param.7), kind=kOutput, calls=%fused_computation | convolution fusion | flops 339738624 | bytes 3538944 | tf_op jit(solution)/shard_map/dot_general | solution.py:22
  82.7 2.4 %fusion.4 = f32[128,1152]{1,0:T(8,128)S(1)} fusion(bf16[128,1152]{1,0:T(8,128)(2,1)S(1)} %bitcast.122, bf16[1,1,2,1152,1152]{4,3,2,1,0:T(8,128)(2,1)} %param.7), kind=kOutput, calls=%fused_computation.4 | convolution fusion | flops 339738624 | bytes 3538944 | tf_op jit(solution)/shard_map/dot_general | solution.py:19
  85.4 0.2 fusion.77
  85.6 1.3 collective-permute-start.6
  87.1 0.2 fusion.78
  87.3 1.3 collective-permute-start.4
  88.6 0.2 collective-permute-done.6
  88.8 0.3 fusion.31
  89.1 0.3 fusion.29
  89.3 4.7 %collective-permute-done.4 = bf16[2,64,192]{2,1,0:T(8,128)(2,1)S(1)} collective-permute-done((bf16[2,64,192]{2,1,0:T(8,128)(2,1)S(1)}, bf16[2,64,192]{2,1,0:T(8,128)(2,1)S(1)}, u32[]{:S(2)}, u32[]{:S(2)}) %collective-permute-start.4) | collective-permute-done | bytes 49184 | tf_op jit(solution)/shard_map/ppermute | solution.py:13
  94.0 0.3 fusion.27
  94.3 0.3 fusion.25
  94.7 2.0 %collective-permute-start.7 = (f32[2,64,192]{2,1,0:T(8,128)S(1)}, f32[2,64,192]{2,1,0:T(8,128)S(1)}, u32[]{:S(2)}, u32[]{:S(2)}) collective-permute-start(f32[2,64,192]{2,1,0:T(8,128)S(1)} %get-tuple-element.40), channel_id=1, source_target_pairs={{0,2},{2,4},{4,6},{1,3},{3,5},{5,7},{8,10},{10,12},{12,14},{9,11},... | collective-permute-start | bytes 294920 | tf_op jit(solution)/shard_map/ppermute | solution.py:13
  96.9 1.7 %collective-permute-start.5 = (f32[2,64,192]{2,1,0:T(8,128)S(1)}, f32[2,64,192]{2,1,0:T(8,128)S(1)}, u32[]{:S(2)}, u32[]{:S(2)}) collective-permute-start(f32[2,64,192]{2,1,0:T(8,128)S(1)} %get-tuple-element.42), channel_id=1, source_target_pairs={{0,8},{8,16},{16,24},{1,9},{9,17},{17,25},{2,10},{10,18},{18,26},{... | collective-permute-start | bytes 294920 | tf_op jit(solution)/shard_map/ppermute | solution.py:13
  98.6 3.6 %collective-permute-done.5 = f32[2,64,192]{2,1,0:T(8,128)S(1)} collective-permute-done((f32[2,64,192]{2,1,0:T(8,128)S(1)}, f32[2,64,192]{2,1,0:T(8,128)S(1)}, u32[]{:S(2)}, u32[]{:S(2)}) %collective-permute-start.5) | collective-permute-done | bytes 98336 | tf_op jit(solution)/shard_map/ppermute | solution.py:13
  102.3 0.2 concatenate.69
  102.5 0.2 multiply_reduce_fusion.1
  102.6 0.6 convolution_bitcast_fusion
  103.2 18.1 %all-gather.3 = f32[16,64,32]{1,2,0:T(8,128)S(1)} all-gather(f32[1,64,32]{1,2,0:T(8,128)S(1)} %convolution_bitcast_fusion), channel_id=3, replica_groups=mesh['gx'=4,'gy'=4,'col'=2] {'gx','gy'}, dimensions={0}, use_global_device_ids=true | all-gather | bytes 139264 | tf_op jit(solution)/shard_map/all_gather | solution.py:84
  121.4 0.5 fusion.34
  121.9 0.8 multiply_reduce_fusion
  122.7 31.2 %all-reduce = (f32[64]{0:T(128)S(1)}, f32[64]{0:T(128)S(1)}) all-reduce(f32[64]{0:T(128)S(1)} %multiply_reduce_fusion.1, f32[64]{0:T(128)S(1)} %get-tuple-element.59), channel_id=1, replica_groups=mesh['gx'=4,'gy'=4,'col'=2] {'gx','gy'}, use_global_device_ids=true, to_apply=%region_5.6 | all-reduce | flops 128 | bytes 1024 | tf_op jit(solution)/shard_map/psum | solution.py:87
  153.8 0.9 fusion.18
  (52 shorter events, 2.2 us)
Async XLA Ops:
  0.0 27.4 %copy-start = (f32[1,1,32,2,1152]{4,3,2,1,0:T(2,128)S(1)}, f32[1,1,32,2,1152]{4,3,2,1,0:T(2,128)}, u32[]{:S(2)}) copy-start(f32[1,1,32,2,1152]{4,3,2,1,0:T(2,128)} %param.10) | copy-start | bytes 884740
  2.4 2.5 %copy-start.2 = (f32[1,1,2,64,1152]{4,3,2,1,0:T(8,128)S(1)}, f32[1,1,2,64,1152]{4,3,2,1,0:T(8,128)}, u32[]{:S(2)}) copy-start(f32[1,1,2,64,1152]{4,3,2,1,0:T(8,128)} %param.6) | copy-start | bytes 1769476
  4.8 4.1 %copy-start.1 = (bf16[1,1,2,2,384,384]{5,4,3,2,1,0:T(8,128)(2,1)S(1)}, bf16[1,1,2,2,384,384]{5,4,3,2,1,0:T(8,128)(2,1)}, u32[]{:S(2)}) copy-start(bf16[1,1,2,2,384,384]{5,4,3,2,1,0:T(8,128)(2,1)} %param.8) | copy-start | bytes 3538948
  5.0 4.1 %copy-start.6 = (s32[1,1,2]{2,1,0:T(1,128)S(1)}, s32[1,1,2]{2,1,0:T(1,128)}, u32[]{:S(2)}) copy-start(s32[1,1,2]{2,1,0:T(1,128)} %param.9) | copy-start | bytes 28
  6.0 6.2 %collective-permute-start.2 = (bf16[2,64,192]{2,1,0:T(8,128)(2,1)S(1)}, bf16[2,64,192]{2,1,0:T(8,128)(2,1)S(1)}, u32[]{:S(2)}, u32[]{:S(2)}) collective-permute-start(bf16[2,64,192]{2,1,0:T(8,128)(2,1)S(1)} %bitcast.131), channel_id=1, source_target_pairs={{2,0},{4,2},{6,4},{3,1},{5,3},{7,5},{10,8},{12,10},{14,12},{11,9},... | collective-permute-start | bytes 147464 | tf_op jit(solution)/shard_map/ppermute | solution.py:13
  7.6 7.5 %collective-permute-start = (bf16[2,64,192]{2,1,0:T(8,128)(2,1)S(1)}, bf16[2,64,192]{2,1,0:T(8,128)(2,1)S(1)}, u32[]{:S(2)}, u32[]{:S(2)}) collective-permute-start(bf16[2,64,192]{2,1,0:T(8,128)(2,1)S(1)} %bitcast.132), channel_id=1, source_target_pairs={{8,0},{16,8},{24,16},{9,1},{17,9},{25,17},{10,2},{18,10},{26,18},{... | collective-permute-start | bytes 147464 | tf_op jit(solution)/shard_map/ppermute | solution.py:13
  11.2 0.9 copy-start.4
  12.1 10.2 %copy-start.5 = (f32[16,512]{1,0:T(8,128)S(1)}, f32[16,512]{1,0:T(8,128)}, u32[]{:S(2)}) copy-start(f32[16,512]{1,0:T(8,128)} %param.11) | copy-start | bytes 98308
  15.8 11.2 %collective-permute-start.3 = (f32[2,64,192]{2,1,0:T(8,128)S(1)}, f32[2,64,192]{2,1,0:T(8,128)S(1)}, u32[]{:S(2)}, u32[]{:S(2)}) collective-permute-start(f32[2,64,192]{2,1,0:T(8,128)S(1)} %get-tuple-element.44), channel_id=1, source_target_pairs={{0,2},{2,4},{4,6},{1,3},{3,5},{5,7},{8,10},{10,12},{12,14},{9,11},... | collective-permute-start | bytes 294920 | tf_op jit(solution)/shard_map/ppermute | solution.py:13
  18.1 8.9 %collective-permute-start.1 = (f32[2,64,192]{2,1,0:T(8,128)S(1)}, f32[2,64,192]{2,1,0:T(8,128)S(1)}, u32[]{:S(2)}, u32[]{:S(2)}) collective-permute-start(f32[2,64,192]{2,1,0:T(8,128)S(1)} %get-tuple-element.46), channel_id=1, source_target_pairs={{0,8},{8,16},{16,24},{1,9},{9,17},{17,25},{2,10},{10,18},{18,26},{... | collective-permute-start | bytes 294920 | tf_op jit(solution)/shard_map/ppermute | solution.py:13
  82.7 2.5 %copy-start.3 = (f32[1,1,2,64,1152]{4,3,2,1,0:T(8,128)S(1)}, f32[1,1,2,64,1152]{4,3,2,1,0:T(8,128)}, u32[]{:S(2)}) copy-start(f32[1,1,2,64,1152]{4,3,2,1,0:T(8,128)} %param.6) | copy-start | bytes 1769476
  85.6 3.1 %collective-permute-start.6 = (bf16[2,64,192]{2,1,0:T(8,128)(2,1)S(1)}, bf16[2,64,192]{2,1,0:T(8,128)(2,1)S(1)}, u32[]{:S(2)}, u32[]{:S(2)}) collective-permute-start(bf16[2,64,192]{2,1,0:T(8,128)(2,1)S(1)} %bitcast.133), channel_id=1, source_target_pairs={{2,0},{4,2},{6,4},{3,1},{5,3},{7,5},{10,8},{12,10},{14,12},{11,9},... | collective-permute-start | bytes 147464 | tf_op jit(solution)/shard_map/ppermute | solution.py:13
  87.3 6.7 %collective-permute-start.4 = (bf16[2,64,192]{2,1,0:T(8,128)(2,1)S(1)}, bf16[2,64,192]{2,1,0:T(8,128)(2,1)S(1)}, u32[]{:S(2)}, u32[]{:S(2)}) collective-permute-start(bf16[2,64,192]{2,1,0:T(8,128)(2,1)S(1)} %bitcast.134), channel_id=1, source_target_pairs={{8,0},{16,8},{24,16},{9,1},{17,9},{25,17},{10,2},{18,10},{26,18},{... | collective-permute-start | bytes 147464 | tf_op jit(solution)/shard_map/ppermute | solution.py:13
  94.7 4.0 %collective-permute-start.7 = (f32[2,64,192]{2,1,0:T(8,128)S(1)}, f32[2,64,192]{2,1,0:T(8,128)S(1)}, u32[]{:S(2)}, u32[]{:S(2)}) collective-permute-start(f32[2,64,192]{2,1,0:T(8,128)S(1)} %get-tuple-element.40), channel_id=1, source_target_pairs={{0,2},{2,4},{4,6},{1,3},{3,5},{5,7},{8,10},{10,12},{12,14},{9,11},... | collective-permute-start | bytes 294920 | tf_op jit(solution)/shard_map/ppermute | solution.py:13
  96.9 5.4 %collective-permute-start.5 = (f32[2,64,192]{2,1,0:T(8,128)S(1)}, f32[2,64,192]{2,1,0:T(8,128)S(1)}, u32[]{:S(2)}, u32[]{:S(2)}) collective-permute-start(f32[2,64,192]{2,1,0:T(8,128)S(1)} %get-tuple-element.42), channel_id=1, source_target_pairs={{0,8},{8,16},{16,24},{1,9},{9,17},{17,25},{2,10},{10,18},{18,26},{... | collective-permute-start | bytes 294920 | tf_op jit(solution)/shard_map/ppermute | solution.py:13
where the time goes:
time: 155 us
  blocking collectives  105 us (68%)
  matrix products  15.5 us (10%)
  starting transfers between devices  15.2 us (10%)
  waiting for transfers between devices  10.8 us (7%)
  local copies, waits for them, and re-layouts  3.56 us (2%)
  other arithmetic  3.24 us (2%)
  between operations  1.81 us (1%)
    psum x2, blocking collectives, per_device(): lax.psum((jnp.sum(defect * defect, axis=(0, 2)), jnp.sum(correction * cor...  61 us
    all_gather x2, blocking collectives, per_device(): gathered = lax.all_gather(projected[None], ('gx', 'gy'), axis=0, tiled=True)  39.2 us
    ppermute x8, starting transfers between devices, shifted(): return lax.ppermute(block, axis, route)  15.2 us
    ppermute x8, waiting for transfers between devices, shifted(): return lax.ppermute(block, axis, route)  10.8 us
    dot_general x6, matrix products, complex_apply(): jnp.dot(flattened, real_part, preferred_element_type=jnp.float32)  5.88 us
    dot_general x6, matrix products, complex_apply(): jnp.dot(flattened, imag_part, preferred_element_type=jnp.float32)  5.81 us
    all_gather x1, blocking collectives, per_device(): pair_rows = lax.all_gather(coarse_inverse, 'col', axis=0, tiled=True)  4.58 us
  transfers between devices with their start and end apart: 8, of which 4 were waited for; matrix products, arithmetic and copies ran while one was open for 3% of the time, Pallas kernels for 0%

commit v1 on v0

--- a/solution.py
+++ b/solution.py
@@ -81,8 +81,27 @@
         )
         defect = updated - iterate
         projected = jnp.einsum("csk,pck->sp", defect, basis_here, precision=lax.Precision.HIGHEST)
-        gathered = lax.all_gather(projected[None], ("gx", "gy"), axis=0, tiled=True)
-        coarse = jnp.einsum("nsp,qnp->sq", gathered, row_blocks, precision=lax.Precision.HIGHEST)
+        length, place = (lax.axis_size(("gx", "gy")), lax.axis_index(("gx", "gy")))
+        downward = [(i_2, (i_2 - 1) % length) for i_2 in range(length)]
+        rows = projected[None].shape[0]
+        block_2 = projected[None]
+        subtotal = jnp.einsum(
+            "nsp,qnp->sq",
+            block_2,
+            lax.dynamic_slice_in_dim(row_blocks, place * rows, block_2.shape[0], axis=1),
+            precision=lax.Precision.HIGHEST,
+        )
+        for step in range(1, length):
+            block_2 = lax.ppermute(block_2, ("gx", "gy"), downward)
+            subtotal = subtotal + jnp.einsum(
+                "nsp,qnp->sq",
+                block_2,
+                lax.dynamic_slice_in_dim(
+                    row_blocks, (place + step) % length * rows, block_2.shape[0], axis=1
+                ),
+                precision=lax.Precision.HIGHEST,
+            )
+        coarse = subtotal
         correction = jnp.einsum("sp,pck->csk", coarse, basis_here, precision=lax.Precision.HIGHEST)
         defect_norm, correction_norm = lax.psum(
             (jnp.sum(defect * defect, axis=(0, 2)), jnp.sum(correction * correction, axis=(0, 2))),

time: 155 us -> 293 us (1.89)
  starting transfers between devices: 15.2 us -> 143 us
  waiting for transfers between devices: 10.8 us -> 49 us
  blocking collectives: 105 us -> 73.3 us
  matrix products: 15.5 us -> 18.7 us
    ppermute x0 -> x30, starting transfers between devices: none -> 127 us  [per_device(): block_2 = lax.ppermute(block_2, ('gx', 'gy'), downward)]
    ppermute x0 -> x30, waiting for transfers between devices: none -> 39.2 us  [per_device(): block_2 = lax.ppermute(block_2, ('gx', 'gy'), downward)]
    all_gather x2 -> x0, blocking collectives: 39.2 us -> none  [per_device(): gathered = lax.all_gather(projected[None], ('gx', 'gy'), axis=0, tiled=True)]
    psum x2, blocking collectives: 61 us -> 67.8 us  [per_device(): lax.psum((jnp.sum(defect * defect, axis=(0, 2)), jnp.sum(correction * cor...]
    dot_general x2 -> x32, matrix products: 1.05 us -> 4.29 us  [the longest x30 4.02 us: per_device(): jnp.einsum('nsp,qnp->sq', block_2, lax.dynamic_slice_in_dim(row_blocks, (...]
  transfers between devices with their start and end apart: 8 -> 38, of which waited for: 4 -> 34; matrix products, arithmetic and copies ran while one was open for 3% -> 3% of each run, Pallas kernels for 0% -> 0%
where the time goes in v1:
time: 293 us; the launch traced here: 292 us
  starting transfers between devices  143 us (49%)
  blocking collectives  73.3 us (25%)
  waiting for transfers between devices  49 us (17%)
  matrix products  18.7 us (6%)
  other arithmetic  3.24 us (1%)
  local copies, waits for them, and re-layouts  3.03 us (1%)
    ppermute x30, starting transfers between devices, per_device(): block_2 = lax.ppermute(block_2, ('gx', 'gy'), downward)  127 us
    psum x2, blocking collectives, per_device(): lax.psum((jnp.sum(defect * defect, axis=(0, 2)), jnp.sum(correction * cor...  67.8 us
    ppermute x30, waiting for transfers between devices, per_device(): block_2 = lax.ppermute(block_2, ('gx', 'gy'), downward)  39.2 us
    ppermute x8, starting transfers between devices, shifted(): return lax.ppermute(block, axis, route)  15.8 us
    ppermute x8, waiting for transfers between devices, shifted(): return lax.ppermute(block, axis, route)  9.83 us
    dot_general x6, matrix products, complex_apply(): jnp.dot(flattened, real_part, preferred_element_type=jnp.float32)  5.88 us
  transfers between devices with their start and end apart: 38, of which 34 were waited for; matrix products, arithmetic and copies ran while one was open for 3% of the time, Pallas kernels for 0%

profile of v1, /device:TPU:0, one launch (start us, length us, event | category | flops | bytes accessed | tf_op | source)
XLA Modules:
  0.0 292.4 jit_solution(12349488715416393359)
XLA Ops:
  0.0 2.4 fusion.2
  2.4 2.4 fusion.6
  11.8 5.5 %all_gather.3 = f32[32,512]{1,0:T(8,128)S(1)} all-gather(f32[16,512]{1,0:T(8,128)S(1)} %copy-done.4), channel_id=1, replica_groups=mesh['gx'=4,'gy'=4,'col'=2] {'col'}, dimensions={0}, use_global_device_ids=true | all-gather | bytes 98304 | tf_op jit(solution)/shard_map/all_gather | solution.py:51
  18.7 2.2 collective-permute-start.3
  21.0 4.7 %collective-permute-start.1 = (f32[2,64,192]{2,1,0:T(8,128)S(1)}, f32[2,64,192]{2,1,0:T(8,128)S(1)}, u32[]{:S(2)}, u32[]{:S(2)}) collective-permute-start(f32[2,64,192]{2,1,0:T(8,128)S(1)} %get-tuple-element.62), channel_id=1, source_target_pairs={{0,8},{8,16},{16,24},{1,9},{9,17},{17,25},{2,10},{10,18},{18,26},{... | collective-permute-start | bytes 294920 | tf_op jit(solution)/shard_map/ppermute | solution.py:13
  26.1 2.2 collective-permute-done.1
  29.2 3.3 %collective-permute-start.4 = (f32[1,64,32]{1,2,0:T(8,128)S(1)}, f32[1,64,32]{1,2,0:T(8,128)S(1)}, u32[]{:S(2)}, u32[]{:S(2)}) collective-permute-start(f32[1,64,32]{1,2,0:T(8,128)S(1)} %bitcast.304), channel_id=1, source_target_pairs={{0,30},{2,0},{4,2},{6,4},{8,6},{10,8},{12,10},{14,12},{16,14},{18,... | collective-permute-start | bytes 24584 | tf_op jit(solution)/shard_map/ppermute | solution.py:95
  34.0 4.4 %collective-permute-start.5 = (f32[1,64,32]{1,2,0:T(8,128)S(1)}, f32[1,64,32]{1,2,0:T(8,128)S(1)}, u32[]{:S(2)}, u32[]{:S(2)}) collective-permute-start(f32[1,64,32]{1,2,0:T(8,128)S(1)} %collective-permute-done.4), channel_id=1, source_target_pairs={{0,30},{2,0},{4,2},{6,4},{8,6},{10,8},{12,10},{14,12},{16,14},{18,... | collective-permute-start | bytes 24584 | tf_op jit(solution)/shard_map/ppermute | solution.py:95
  38.5 1.3 collective-permute-done.5
  39.8 4.4 %collective-permute-start.6 = (f32[1,64,32]{1,2,0:T(8,128)S(1)}, f32[1,64,32]{1,2,0:T(8,128)S(1)}, u32[]{:S(2)}, u32[]{:S(2)}) collective-permute-start(f32[1,64,32]{1,2,0:T(8,128)S(1)} %collective-permute-done.5), channel_id=1, source_target_pairs={{0,30},{2,0},{4,2},{6,4},{8,6},{10,8},{12,10},{14,12},{16,14},{18,... | collective-permute-start | bytes 24584 | tf_op jit(solution)/shard_map/ppermute | solution.py:95
  44.4 1.3 collective-permute-done.6
  45.7 4.4 %collective-permute-start.7 = (f32[1,64,32]{1,2,0:T(8,128)S(1)}, f32[1,64,32]{1,2,0:T(8,128)S(1)}, u32[]{:S(2)}, u32[]{:S(2)}) collective-permute-start(f32[1,64,32]{1,2,0:T(8,128)S(1)} %collective-permute-done.6), channel_id=1, source_target_pairs={{0,30},{2,0},{4,2},{6,4},{8,6},{10,8},{12,10},{14,12},{16,14},{18,... | collective-permute-start | bytes 24584 | tf_op jit(solution)/shard_map/ppermute | solution.py:95
  50.2 1.3 collective-permute-done.7
  51.5 4.4 %collective-permute-start.8 = (f32[1,64,32]{1,2,0:T(8,128)S(1)}, f32[1,64,32]{1,2,0:T(8,128)S(1)}, u32[]{:S(2)}, u32[]{:S(2)}) collective-permute-start(f32[1,64,32]{1,2,0:T(8,128)S(1)} %collective-permute-done.7), channel_id=1, source_target_pairs={{0,30},{2,0},{4,2},{6,4},{8,6},{10,8},{12,10},{14,12},{16,14},{18,... | collective-permute-start | bytes 24584 | tf_op jit(solution)/shard_map/ppermute | solution.py:95
  57.4 4.4 %collective-permute-start.9 = (f32[1,64,32]{1,2,0:T(8,128)S(1)}, f32[1,64,32]{1,2,0:T(8,128)S(1)}, u32[]{:S(2)}, u32[]{:S(2)}) collective-permute-start(f32[1,64,32]{1,2,0:T(8,128)S(1)} %collective-permute-done.8), channel_id=1, source_target_pairs={{0,30},{2,0},{4,2},{6,4},{8,6},{10,8},{12,10},{14,12},{16,14},{18,... | collective-permute-start | bytes 24584 | tf_op jit(solution)/shard_map/ppermute | solution.py:95
  63.3 4.4 %collective-permute-start.10 = (f32[1,64,32]{1,2,0:T(8,128)S(1)}, f32[1,64,32]{1,2,0:T(8,128)S(1)}, u32[]{:S(2)}, u32[]{:S(2)}) collective-permute-start(f32[1,64,32]{1,2,0:T(8,128)S(1)} %collective-permute-done.9), channel_id=1, source_target_pairs={{0,30},{2,0},{4,2},{6,4},{8,6},{10,8},{12,10},{14,12},{16,14},{18,... | collective-permute-start | bytes 24584 | tf_op jit(solution)/shard_map/ppermute | solution.py:95
  69.1 4.4 %collective-permute-start.11 = (f32[1,64,32]{1,2,0:T(8,128)S(1)}, f32[1,64,32]{1,2,0:T(8,128)S(1)}, u32[]{:S(2)}, u32[]{:S(2)}) collective-permute-start(f32[1,64,32]{1,2,0:T(8,128)S(1)} %collective-permute-done.10), channel_id=1, source_target_pairs={{0,30},{2,0},{4,2},{6,4},{8,6},{10,8},{12,10},{14,12},{16,14},{18,... | collective-permute-start | bytes 24584 | tf_op jit(solution)/shard_map/ppermute | solution.py:95
  75.0 4.4 %collective-permute-start.12 = (f32[1,64,32]{1,2,0:T(8,128)S(1)}, f32[1,64,32]{1,2,0:T(8,128)S(1)}, u32[]{:S(2)}, u32[]{:S(2)}) collective-permute-start(f32[1,64,32]{1,2,0:T(8,128)S(1)} %collective-permute-done.11), channel_id=1, source_target_pairs={{0,30},{2,0},{4,2},{6,4},{8,6},{10,8},{12,10},{14,12},{16,14},{18,... | collective-permute-start | bytes 24584 | tf_op jit(solution)/shard_map/ppermute | solution.py:95
  79.5 1.3 collective-permute-done.12
  80.8 4.4 %collective-permute-start.13 = (f32[1,64,32]{1,2,0:T(8,128)S(1)}, f32[1,64,32]{1,2,0:T(8,128)S(1)}, u32[]{:S(2)}, u32[]{:S(2)}) collective-permute-start(f32[1,64,32]{1,2,0:T(8,128)S(1)} %collective-permute-done.12), channel_id=1, source_target_pairs={{0,30},{2,0},{4,2},{6,4},{8,6},{10,8},{12,10},{14,12},{16,14},{18,... | collective-permute-start | bytes 24584 | tf_op jit(solution)/shard_map/ppermute | solution.py:95
  85.4 1.3 collective-permute-done.13
  86.7 4.4 %collective-permute-start.14 = (f32[1,64,32]{1,2,0:T(8,128)S(1)}, f32[1,64,32]{1,2,0:T(8,128)S(1)}, u32[]{:S(2)}, u32[]{:S(2)}) collective-permute-start(f32[1,64,32]{1,2,0:T(8,128)S(1)} %collective-permute-done.13), channel_id=1, source_target_pairs={{0,30},{2,0},{4,2},{6,4},{8,6},{10,8},{12,10},{14,12},{16,14},{18,... | collective-permute-start | bytes 24584 | tf_op jit(solution)/shard_map/ppermute | solution.py:95
  92.6 4.4 %collective-permute-start.15 = (f32[1,64,32]{1,2,0:T(8,128)S(1)}, f32[1,64,32]{1,2,0:T(8,128)S(1)}, u32[]{:S(2)}, u32[]{:S(2)}) collective-permute-start(f32[1,64,32]{1,2,0:T(8,128)S(1)} %collective-permute-done.14), channel_id=1, source_target_pairs={{0,30},{2,0},{4,2},{6,4},{8,6},{10,8},{12,10},{14,12},{16,14},{18,... | collective-permute-start | bytes 24584 | tf_op jit(solution)/shard_map/ppermute | solution.py:95
  98.4 4.4 %collective-permute-start.16 = (f32[1,64,32]{1,2,0:T(8,128)S(1)}, f32[1,64,32]{1,2,0:T(8,128)S(1)}, u32[]{:S(2)}, u32[]{:S(2)}) collective-permute-start(f32[1,64,32]{1,2,0:T(8,128)S(1)} %collective-permute-done.15), channel_id=1, source_target_pairs={{0,30},{2,0},{4,2},{6,4},{8,6},{10,8},{12,10},{14,12},{16,14},{18,... | collective-permute-start | bytes 24584 | tf_op jit(solution)/shard_map/ppermute | solution.py:95
  104.3 4.4 %collective-permute-start.17 = (f32[1,64,32]{1,2,0:T(8,128)S(1)}, f32[1,64,32]{1,2,0:T(8,128)S(1)}, u32[]{:S(2)}, u32[]{:S(2)}) collective-permute-start(f32[1,64,32]{1,2,0:T(8,128)S(1)} %collective-permute-done.16), channel_id=1, source_target_pairs={{0,30},{2,0},{4,2},{6,4},{8,6},{10,8},{12,10},{14,12},{16,14},{18,... | collective-permute-start | bytes 24584 | tf_op jit(solution)/shard_map/ppermute | solution.py:95
  110.2 4.4 %collective-permute-start.18 = (f32[1,64,32]{1,2,0:T(8,128)S(1)}, f32[1,64,32]{1,2,0:T(8,128)S(1)}, u32[]{:S(2)}, u32[]{:S(2)}) collective-permute-start(f32[1,64,32]{1,2,0:T(8,128)S(1)} %collective-permute-done.17), channel_id=1, source_target_pairs={{0,30},{2,0},{4,2},{6,4},{8,6},{10,8},{12,10},{14,12},{16,14},{18,... | collective-permute-start | bytes 24584 | tf_op jit(solution)/shard_map/ppermute | solution.py:95
  116.9 33.9 %all-reduce.1 = (f32[64]{0:T(128)S(1)}, f32[64]{0:T(128)S(1)}) all-reduce(f32[64]{0:T(128)S(1)} %multiply_reduce_fusion.3, f32[64]{0:T(128)S(1)} %get-tuple-element.73), channel_id=1, replica_groups=mesh['gx'=4,'gy'=4,'col'=2] {'gx','gy'}, use_global_device_ids=true, to_apply=%region_1.2 | all-reduce | flops 128 | bytes 1024 | tf_op jit(solution)/shard_map/psum | solution.py:106
  151.0 2.3 fusion
  153.4 2.4 fusion.4
  160.0 4.7 %collective-permute-done.19 = bf16[2,64,192]{2,1,0:T(8,128)(2,1)S(1)} collective-permute-done((bf16[2,64,192]{2,1,0:T(8,128)(2,1)S(1)}, bf16[2,64,192]{2,1,0:T(8,128)(2,1)S(1)}, u32[]{:S(2)}, u32[]{:S(2)}) %collective-permute-start.19) | collective-permute-done | bytes 49184 | tf_op jit(solution)/shard_map/ppermute | solution.py:13
  165.3 2.0 collective-permute-start.22
  167.5 1.7 collective-permute-start.20
  169.3 2.8 collective-permute-done.20
  174.5 4.4 %collective-permute-start.24 = (f32[1,64,32]{1,2,0:T(8,128)S(1)}, f32[1,64,32]{1,2,0:T(8,128)S(1)}, u32[]{:S(2)}, u32[]{:S(2)}) collective-permute-start(f32[1,64,32]{1,2,0:T(8,128)S(1)} %collective-permute-done.23), channel_id=1, source_target_pairs={{0,30},{2,0},{4,2},{6,4},{8,6},{10,8},{12,10},{14,12},{16,14},{18,... | collective-permute-start | bytes 24584 | tf_op jit(solution)/shard_map/ppermute | solution.py:95
  180.4 4.4 %collective-permute-start.25 = (f32[1,64,32]{1,2,0:T(8,128)S(1)}, f32[1,64,32]{1,2,0:T(8,128)S(1)}, u32[]{:S(2)}, u32[]{:S(2)}) collective-permute-start(f32[1,64,32]{1,2,0:T(8,128)S(1)} %collective-permute-done.24), channel_id=1, source_target_pairs={{0,30},{2,0},{4,2},{6,4},{8,6},{10,8},{12,10},{14,12},{16,14},{18,... | collective-permute-start | bytes 24584 | tf_op jit(solution)/shard_map/ppermute | solution.py:95
  186.2 4.4 %collective-permute-start.26 = (f32[1,64,32]{1,2,0:T(8,128)S(1)}, f32[1,64,32]{1,2,0:T(8,128)S(1)}, u32[]{:S(2)}, u32[]{:S(2)}) collective-permute-start(f32[1,64,32]{1,2,0:T(8,128)S(1)} %collective-permute-done.25), channel_id=1, source_target_pairs={{0,30},{2,0},{4,2},{6,4},{8,6},{10,8},{12,10},{14,12},{16,14},{18,... | collective-permute-start | bytes 24584 | tf_op jit(solution)/shard_map/ppermute | solution.py:95
  192.1 4.4 %collective-permute-start.27 = (f32[1,64,32]{1,2,0:T(8,128)S(1)}, f32[1,64,32]{1,2,0:T(8,128)S(1)}, u32[]{:S(2)}, u32[]{:S(2)}) collective-permute-start(f32[1,64,32]{1,2,0:T(8,128)S(1)} %collective-permute-done.26), channel_id=1, source_target_pairs={{0,30},{2,0},{4,2},{6,4},{8,6},{10,8},{12,10},{14,12},{16,14},{18,... | collective-permute-start | bytes 24584 | tf_op jit(solution)/shard_map/ppermute | solution.py:95
  198.0 4.4 %collective-permute-start.28 = (f32[1,64,32]{1,2,0:T(8,128)S(1)}, f32[1,64,32]{1,2,0:T(8,128)S(1)}, u32[]{:S(2)}, u32[]{:S(2)}) collective-permute-start(f32[1,64,32]{1,2,0:T(8,128)S(1)} %collective-permute-done.27), channel_id=1, source_target_pairs={{0,30},{2,0},{4,2},{6,4},{8,6},{10,8},{12,10},{14,12},{16,14},{18,... | collective-permute-start | bytes 24584 | tf_op jit(solution)/shard_map/ppermute | solution.py:95
  203.8 4.4 %collective-permute-start.29 = (f32[1,64,32]{1,2,0:T(8,128)S(1)}, f32[1,64,32]{1,2,0:T(8,128)S(1)}, u32[]{:S(2)}, u32[]{:S(2)}) collective-permute-start(f32[1,64,32]{1,2,0:T(8,128)S(1)} %collective-permute-done.28), channel_id=1, source_target_pairs={{0,30},{2,0},{4,2},{6,4},{8,6},{10,8},{12,10},{14,12},{16,14},{18,... | collective-permute-start | bytes 24584 | tf_op jit(solution)/shard_map/ppermute | solution.py:95
  209.7 4.4 %collective-permute-start.30 = (f32[1,64,32]{1,2,0:T(8,128)S(1)}, f32[1,64,32]{1,2,0:T(8,128)S(1)}, u32[]{:S(2)}, u32[]{:S(2)}) collective-permute-start(f32[1,64,32]{1,2,0:T(8,128)S(1)} %collective-permute-done.29), channel_id=1, source_target_pairs={{0,30},{2,0},{4,2},{6,4},{8,6},{10,8},{12,10},{14,12},{16,14},{18,... | collective-permute-start | bytes 24584 | tf_op jit(solution)/shard_map/ppermute | solution.py:95
  215.6 4.4 %collective-permute-start.31 = (f32[1,64,32]{1,2,0:T(8,128)S(1)}, f32[1,64,32]{1,2,0:T(8,128)S(1)}, u32[]{:S(2)}, u32[]{:S(2)}) collective-permute-start(f32[1,64,32]{1,2,0:T(8,128)S(1)} %collective-permute-done.30), channel_id=1, source_target_pairs={{0,30},{2,0},{4,2},{6,4},{8,6},{10,8},{12,10},{14,12},{16,14},{18,... | collective-permute-start | bytes 24584 | tf_op jit(solution)/shard_map/ppermute | solution.py:95
  221.4 4.4 %collective-permute-start.32 = (f32[1,64,32]{1,2,0:T(8,128)S(1)}, f32[1,64,32]{1,2,0:T(8,128)S(1)}, u32[]{:S(2)}, u32[]{:S(2)}) collective-permute-start(f32[1,64,32]{1,2,0:T(8,128)S(1)} %collective-permute-done.31), channel_id=1, source_target_pairs={{0,30},{2,0},{4,2},{6,4},{8,6},{10,8},{12,10},{14,12},{16,14},{18,... | collective-permute-start | bytes 24584 | tf_op jit(solution)/shard_map/ppermute | solution.py:95
  227.3 4.4 %collective-permute-start.33 = (f32[1,64,32]{1,2,0:T(8,128)S(1)}, f32[1,64,32]{1,2,0:T(8,128)S(1)}, u32[]{:S(2)}, u32[]{:S(2)}) collective-permute-start(f32[1,64,32]{1,2,0:T(8,128)S(1)} %collective-permute-done.32), channel_id=1, source_target_pairs={{0,30},{2,0},{4,2},{6,4},{8,6},{10,8},{12,10},{14,12},{16,14},{18,... | collective-permute-start | bytes 24584 | tf_op jit(solution)/shard_map/ppermute | solution.py:95
  233.1 4.4 %collective-permute-start.34 = (f32[1,64,32]{1,2,0:T(8,128)S(1)}, f32[1,64,32]{1,2,0:T(8,128)S(1)}, u32[]{:S(2)}, u32[]{:S(2)}) collective-permute-start(f32[1,64,32]{1,2,0:T(8,128)S(1)} %collective-permute-done.33), channel_id=1, source_target_pairs={{0,30},{2,0},{4,2},{6,4},{8,6},{10,8},{12,10},{14,12},{16,14},{18,... | collective-permute-start | bytes 24584 | tf_op jit(solution)/shard_map/ppermute | solution.py:95
  239.0 4.4 %collective-permute-start.35 = (f32[1,64,32]{1,2,0:T(8,128)S(1)}, f32[1,64,32]{1,2,0:T(8,128)S(1)}, u32[]{:S(2)}, u32[]{:S(2)}) collective-permute-start(f32[1,64,32]{1,2,0:T(8,128)S(1)} %collective-permute-done.34), channel_id=1, source_target_pairs={{0,30},{2,0},{4,2},{6,4},{8,6},{10,8},{12,10},{14,12},{16,14},{18,... | collective-permute-start | bytes 24584 | tf_op jit(solution)/shard_map/ppermute | solution.py:95
  244.9 4.4 %collective-permute-start.36 = (f32[1,64,32]{1,2,0:T(8,128)S(1)}, f32[1,64,32]{1,2,0:T(8,128)S(1)}, u32[]{:S(2)}, u32[]{:S(2)}) collective-permute-start(f32[1,64,32]{1,2,0:T(8,128)S(1)} %collective-permute-done.35), channel_id=1, source_target_pairs={{0,30},{2,0},{4,2},{6,4},{8,6},{10,8},{12,10},{14,12},{16,14},{18,... | collective-permute-start | bytes 24584 | tf_op jit(solution)/shard_map/ppermute | solution.py:95
  250.7 4.4 %collective-permute-start.37 = (f32[1,64,32]{1,2,0:T(8,128)S(1)}, f32[1,64,32]{1,2,0:T(8,128)S(1)}, u32[]{:S(2)}, u32[]{:S(2)}) collective-permute-start(f32[1,64,32]{1,2,0:T(8,128)S(1)} %collective-permute-done.36), channel_id=1, source_target_pairs={{0,30},{2,0},{4,2},{6,4},{8,6},{10,8},{12,10},{14,12},{16,14},{18,... | collective-permute-start | bytes 24584 | tf_op jit(solution)/shard_map/ppermute | solution.py:95
  257.5 33.9 %all-reduce = (f32[64]{0:T(128)S(1)}, f32[64]{0:T(128)S(1)}) all-reduce(f32[64]{0:T(128)S(1)} %multiply_reduce_fusion.1, f32[64]{0:T(128)S(1)} %get-tuple-element.75), channel_id=1, replica_groups=mesh['gx'=4,'gy'=4,'col'=2] {'gx','gy'}, use_global_device_ids=true, to_apply=%region_5.6 | all-reduce | flops 128 | bytes 1024 | tf_op jit(solution)/shard_map/psum | solution.py:106
  (139 shorter events, 53.5 us)
Async XLA Ops:
  0.0 28.5 %copy-start = (f32[1,1,32,2,1152]{4,3,2,1,0:T(2,128)S(1)}, f32[1,1,32,2,1152]{4,3,2,1,0:T(2,128)}, u32[]{:S(2)}) copy-start(f32[1,1,32,2,1152]{4,3,2,1,0:T(2,128)} %param.10) | copy-start | bytes 884740
  2.4 2.5 copy-start.2
  4.8 3.5 %copy-start.1 = (bf16[1,1,2,2,384,384]{5,4,3,2,1,0:T(8,128)(2,1)S(1)}, bf16[1,1,2,2,384,384]{5,4,3,2,1,0:T(8,128)(2,1)}, u32[]{:S(2)}) copy-start(bf16[1,1,2,2,384,384]{5,4,3,2,1,0:T(8,128)(2,1)} %param.8) | copy-start | bytes 3538948
  5.0 3.5 %copy-start.5 = (s32[1,1,2]{2,1,0:T(1,128)S(1)}, s32[1,1,2]{2,1,0:T(1,128)}, u32[]{:S(2)}) copy-start(s32[1,1,2]{2,1,0:T(1,128)} %param.9) | copy-start | bytes 28
  5.4 12.1 %collective-permute-start.2 = (bf16[2,64,192]{2,1,0:T(8,128)(2,1)S(1)}, bf16[2,64,192]{2,1,0:T(8,128)(2,1)S(1)}, u32[]{:S(2)}, u32[]{:S(2)}) collective-permute-start(bf16[2,64,192]{2,1,0:T(8,128)(2,1)S(1)} %bitcast.305), channel_id=1, source_target_pairs={{2,0},{4,2},{6,4},{3,1},{5,3},{7,5},{10,8},{12,10},{14,12},{11,9},... | collective-permute-start | bytes 147464 | tf_op jit(solution)/shard_map/ppermute | solution.py:13
  7.0 11.0 %collective-permute-start = (bf16[2,64,192]{2,1,0:T(8,128)(2,1)S(1)}, bf16[2,64,192]{2,1,0:T(8,128)(2,1)S(1)}, u32[]{:S(2)}, u32[]{:S(2)}) collective-permute-start(bf16[2,64,192]{2,1,0:T(8,128)(2,1)S(1)} %bitcast.306), channel_id=1, source_target_pairs={{8,0},{16,8},{24,16},{9,1},{17,9},{25,17},{10,2},{18,10},{26,18},{... | collective-permute-start | bytes 147464 | tf_op jit(solution)/shard_map/ppermute | solution.py:13
  10.9 0.9 copy-start.4
  18.7 7.3 %collective-permute-start.3 = (f32[2,64,192]{2,1,0:T(8,128)S(1)}, f32[2,64,192]{2,1,0:T(8,128)S(1)}, u32[]{:S(2)}, u32[]{:S(2)}) collective-permute-start(f32[2,64,192]{2,1,0:T(8,128)S(1)} %get-tuple-element.60), channel_id=1, source_target_pairs={{0,2},{2,4},{4,6},{1,3},{3,5},{5,7},{8,10},{10,12},{12,14},{9,11},... | collective-permute-start | bytes 294920 | tf_op jit(solution)/shard_map/ppermute | solution.py:13
  21.0 7.2 %collective-permute-start.1 = (f32[2,64,192]{2,1,0:T(8,128)S(1)}, f32[2,64,192]{2,1,0:T(8,128)S(1)}, u32[]{:S(2)}, u32[]{:S(2)}) collective-permute-start(f32[2,64,192]{2,1,0:T(8,128)S(1)} %get-tuple-element.62), channel_id=1, source_target_pairs={{0,8},{8,16},{16,24},{1,9},{9,17},{17,25},{2,10},{10,18},{18,26},{... | collective-permute-start | bytes 294920 | tf_op jit(solution)/shard_map/ppermute | solution.py:13
  29.2 4.7 %collective-permute-start.4 = (f32[1,64,32]{1,2,0:T(8,128)S(1)}, f32[1,64,32]{1,2,0:T(8,128)S(1)}, u32[]{:S(2)}, u32[]{:S(2)}) collective-permute-start(f32[1,64,32]{1,2,0:T(8,128)S(1)} %bitcast.304), channel_id=1, source_target_pairs={{0,30},{2,0},{4,2},{6,4},{8,6},{10,8},{12,10},{14,12},{16,14},{18,... | collective-permute-start | bytes 24584 | tf_op jit(solution)/shard_map/ppermute | solution.py:95
  34.0 5.9 %collective-permute-start.5 = (f32[1,64,32]{1,2,0:T(8,128)S(1)}, f32[1,64,32]{1,2,0:T(8,128)S(1)}, u32[]{:S(2)}, u32[]{:S(2)}) collective-permute-start(f32[1,64,32]{1,2,0:T(8,128)S(1)} %collective-permute-done.4), channel_id=1, source_target_pairs={{0,30},{2,0},{4,2},{6,4},{8,6},{10,8},{12,10},{14,12},{16,14},{18,... | collective-permute-start | bytes 24584 | tf_op jit(solution)/shard_map/ppermute | solution.py:95
  39.8 5.9 %collective-permute-start.6 = (f32[1,64,32]{1,2,0:T(8,128)S(1)}, f32[1,64,32]{1,2,0:T(8,128)S(1)}, u32[]{:S(2)}, u32[]{:S(2)}) collective-permute-start(f32[1,64,32]{1,2,0:T(8,128)S(1)} %collective-permute-done.5), channel_id=1, source_target_pairs={{0,30},{2,0},{4,2},{6,4},{8,6},{10,8},{12,10},{14,12},{16,14},{18,... | collective-permute-start | bytes 24584 | tf_op jit(solution)/shard_map/ppermute | solution.py:95
  45.7 5.9 %collective-permute-start.7 = (f32[1,64,32]{1,2,0:T(8,128)S(1)}, f32[1,64,32]{1,2,0:T(8,128)S(1)}, u32[]{:S(2)}, u32[]{:S(2)}) collective-permute-start(f32[1,64,32]{1,2,0:T(8,128)S(1)} %collective-permute-done.6), channel_id=1, source_target_pairs={{0,30},{2,0},{4,2},{6,4},{8,6},{10,8},{12,10},{14,12},{16,14},{18,... | collective-permute-start | bytes 24584 | tf_op jit(solution)/shard_map/ppermute | solution.py:95
  51.5 5.9 %collective-permute-start.8 = (f32[1,64,32]{1,2,0:T(8,128)S(1)}, f32[1,64,32]{1,2,0:T(8,128)S(1)}, u32[]{:S(2)}, u32[]{:S(2)}) collective-permute-start(f32[1,64,32]{1,2,0:T(8,128)S(1)} %collective-permute-done.7), channel_id=1, source_target_pairs={{0,30},{2,0},{4,2},{6,4},{8,6},{10,8},{12,10},{14,12},{16,14},{18,... | collective-permute-start | bytes 24584 | tf_op jit(solution)/shard_map/ppermute | solution.py:95
  57.4 5.9 %collective-permute-start.9 = (f32[1,64,32]{1,2,0:T(8,128)S(1)}, f32[1,64,32]{1,2,0:T(8,128)S(1)}, u32[]{:S(2)}, u32[]{:S(2)}) collective-permute-start(f32[1,64,32]{1,2,0:T(8,128)S(1)} %collective-permute-done.8), channel_id=1, source_target_pairs={{0,30},{2,0},{4,2},{6,4},{8,6},{10,8},{12,10},{14,12},{16,14},{18,... | collective-permute-start | bytes 24584 | tf_op jit(solution)/shard_map/ppermute | solution.py:95
  63.3 5.9 %collective-permute-start.10 = (f32[1,64,32]{1,2,0:T(8,128)S(1)}, f32[1,64,32]{1,2,0:T(8,128)S(1)}, u32[]{:S(2)}, u32[]{:S(2)}) collective-permute-start(f32[1,64,32]{1,2,0:T(8,128)S(1)} %collective-permute-done.9), channel_id=1, source_target_pairs={{0,30},{2,0},{4,2},{6,4},{8,6},{10,8},{12,10},{14,12},{16,14},{18,... | collective-permute-start | bytes 24584 | tf_op jit(solution)/shard_map/ppermute | solution.py:95
  69.1 5.9 %collective-permute-start.11 = (f32[1,64,32]{1,2,0:T(8,128)S(1)}, f32[1,64,32]{1,2,0:T(8,128)S(1)}, u32[]{:S(2)}, u32[]{:S(2)}) collective-permute-start(f32[1,64,32]{1,2,0:T(8,128)S(1)} %collective-permute-done.10), channel_id=1, source_target_pairs={{0,30},{2,0},{4,2},{6,4},{8,6},{10,8},{12,10},{14,12},{16,14},{18,... | collective-permute-start | bytes 24584 | tf_op jit(solution)/shard_map/ppermute | solution.py:95
  75.0 5.9 %collective-permute-start.12 = (f32[1,64,32]{1,2,0:T(8,128)S(1)}, f32[1,64,32]{1,2,0:T(8,128)S(1)}, u32[]{:S(2)}, u32[]{:S(2)}) collective-permute-start(f32[1,64,32]{1,2,0:T(8,128)S(1)} %collective-permute-done.11), channel_id=1, source_target_pairs={{0,30},{2,0},{4,2},{6,4},{8,6},{10,8},{12,10},{14,12},{16,14},{18,... | collective-permute-start | bytes 24584 | tf_op jit(solution)/shard_map/ppermute | solution.py:95
  80.8 5.9 %collective-permute-start.13 = (f32[1,64,32]{1,2,0:T(8,128)S(1)}, f32[1,64,32]{1,2,0:T(8,128)S(1)}, u32[]{:S(2)}, u32[]{:S(2)}) collective-permute-start(f32[1,64,32]{1,2,0:T(8,128)S(1)} %collective-permute-done.12), channel_id=1, source_target_pairs={{0,30},{2,0},{4,2},{6,4},{8,6},{10,8},{12,10},{14,12},{16,14},{18,... | collective-permute-start | bytes 24584 | tf_op jit(solution)/shard_map/ppermute | solution.py:95
  86.7 5.9 %collective-permute-start.14 = (f32[1,64,32]{1,2,0:T(8,128)S(1)}, f32[1,64,32]{1,2,0:T(8,128)S(1)}, u32[]{:S(2)}, u32[]{:S(2)}) collective-permute-start(f32[1,64,32]{1,2,0:T(8,128)S(1)} %collective-permute-done.13), channel_id=1, source_target_pairs={{0,30},{2,0},{4,2},{6,4},{8,6},{10,8},{12,10},{14,12},{16,14},{18,... | collective-permute-start | bytes 24584 | tf_op jit(solution)/shard_map/ppermute | solution.py:95
  92.6 5.9 %collective-permute-start.15 = (f32[1,64,32]{1,2,0:T(8,128)S(1)}, f32[1,64,32]{1,2,0:T(8,128)S(1)}, u32[]{:S(2)}, u32[]{:S(2)}) collective-permute-start(f32[1,64,32]{1,2,0:T(8,128)S(1)} %collective-permute-done.14), channel_id=1, source_target_pairs={{0,30},{2,0},{4,2},{6,4},{8,6},{10,8},{12,10},{14,12},{16,14},{18,... | collective-permute-start | bytes 24584 | tf_op jit(solution)/shard_map/ppermute | solution.py:95
  98.4 5.9 %collective-permute-start.16 = (f32[1,64,32]{1,2,0:T(8,128)S(1)}, f32[1,64,32]{1,2,0:T(8,128)S(1)}, u32[]{:S(2)}, u32[]{:S(2)}) collective-permute-start(f32[1,64,32]{1,2,0:T(8,128)S(1)} %collective-permute-done.15), channel_id=1, source_target_pairs={{0,30},{2,0},{4,2},{6,4},{8,6},{10,8},{12,10},{14,12},{16,14},{18,... | collective-permute-start | bytes 24584 | tf_op jit(solution)/shard_map/ppermute | solution.py:95
  104.3 5.9 %collective-permute-start.17 = (f32[1,64,32]{1,2,0:T(8,128)S(1)}, f32[1,64,32]{1,2,0:T(8,128)S(1)}, u32[]{:S(2)}, u32[]{:S(2)}) collective-permute-start(f32[1,64,32]{1,2,0:T(8,128)S(1)} %collective-permute-done.16), channel_id=1, source_target_pairs={{0,30},{2,0},{4,2},{6,4},{8,6},{10,8},{12,10},{14,12},{16,14},{18,... | collective-permute-start | bytes 24584 | tf_op jit(solution)/shard_map/ppermute | solution.py:95
  110.2 5.9 %collective-permute-start.18 = (f32[1,64,32]{1,2,0:T(8,128)S(1)}, f32[1,64,32]{1,2,0:T(8,128)S(1)}, u32[]{:S(2)}, u32[]{:S(2)}) collective-permute-start(f32[1,64,32]{1,2,0:T(8,128)S(1)} %collective-permute-done.17), channel_id=1, source_target_pairs={{0,30},{2,0},{4,2},{6,4},{8,6},{10,8},{12,10},{14,12},{16,14},{18,... | collective-permute-start | bytes 24584 | tf_op jit(solution)/shard_map/ppermute | solution.py:95
  153.4 2.5 copy-start.3
  156.3 3.1 %collective-permute-start.21 = (bf16[2,64,192]{2,1,0:T(8,128)(2,1)S(1)}, bf16[2,64,192]{2,1,0:T(8,128)(2,1)S(1)}, u32[]{:S(2)}, u32[]{:S(2)}) collective-permute-start(bf16[2,64,192]{2,1,0:T(8,128)(2,1)S(1)} %bitcast.307), channel_id=1, source_target_pairs={{2,0},{4,2},{6,4},{3,1},{5,3},{7,5},{10,8},{12,10},{14,12},{11,9},... | collective-permute-start | bytes 147464 | tf_op jit(solution)/shard_map/ppermute | solution.py:13
  158.0 6.7 %collective-permute-start.19 = (bf16[2,64,192]{2,1,0:T(8,128)(2,1)S(1)}, bf16[2,64,192]{2,1,0:T(8,128)(2,1)S(1)}, u32[]{:S(2)}, u32[]{:S(2)}) collective-permute-start(bf16[2,64,192]{2,1,0:T(8,128)(2,1)S(1)} %bitcast.308), channel_id=1, source_target_pairs={{8,0},{16,8},{24,16},{9,1},{17,9},{25,17},{10,2},{18,10},{26,18},{... | collective-permute-start | bytes 147464 | tf_op jit(solution)/shard_map/ppermute | solution.py:13
  165.3 4.0 %collective-permute-start.22 = (f32[2,64,192]{2,1,0:T(8,128)S(1)}, f32[2,64,192]{2,1,0:T(8,128)S(1)}, u32[]{:S(2)}, u32[]{:S(2)}) collective-permute-start(f32[2,64,192]{2,1,0:T(8,128)S(1)} %get-tuple-element.56), channel_id=1, source_target_pairs={{0,2},{2,4},{4,6},{1,3},{3,5},{5,7},{8,10},{10,12},{12,14},{9,11},... | collective-permute-start | bytes 294920 | tf_op jit(solution)/shard_map/ppermute | solution.py:13
  167.5 4.6 %collective-permute-start.20 = (f32[2,64,192]{2,1,0:T(8,128)S(1)}, f32[2,64,192]{2,1,0:T(8,128)S(1)}, u32[]{:S(2)}, u32[]{:S(2)}) collective-permute-start(f32[2,64,192]{2,1,0:T(8,128)S(1)} %get-tuple-element.58), channel_id=1, source_target_pairs={{0,8},{8,16},{16,24},{1,9},{9,17},{17,25},{2,10},{10,18},{18,26},{... | collective-permute-start | bytes 294920 | tf_op jit(solution)/shard_map/ppermute | solution.py:13
  173.1 1.5 collective-permute-start.23
  174.5 5.9 %collective-permute-start.24 = (f32[1,64,32]{1,2,0:T(8,128)S(1)}, f32[1,64,32]{1,2,0:T(8,128)S(1)}, u32[]{:S(2)}, u32[]{:S(2)}) collective-permute-start(f32[1,64,32]{1,2,0:T(8,128)S(1)} %collective-permute-done.23), channel_id=1, source_target_pairs={{0,30},{2,0},{4,2},{6,4},{8,6},{10,8},{12,10},{14,12},{16,14},{18,... | collective-permute-start | bytes 24584 | tf_op jit(solution)/shard_map/ppermute | solution.py:95
  180.4 5.9 %collective-permute-start.25 = (f32[1,64,32]{1,2,0:T(8,128)S(1)}, f32[1,64,32]{1,2,0:T(8,128)S(1)}, u32[]{:S(2)}, u32[]{:S(2)}) collective-permute-start(f32[1,64,32]{1,2,0:T(8,128)S(1)} %collective-permute-done.24), channel_id=1, source_target_pairs={{0,30},{2,0},{4,2},{6,4},{8,6},{10,8},{12,10},{14,12},{16,14},{18,... | collective-permute-start | bytes 24584 | tf_op jit(solution)/shard_map/ppermute | solution.py:95
  186.2 5.9 %collective-permute-start.26 = (f32[1,64,32]{1,2,0:T(8,128)S(1)}, f32[1,64,32]{1,2,0:T(8,128)S(1)}, u32[]{:S(2)}, u32[]{:S(2)}) collective-permute-start(f32[1,64,32]{1,2,0:T(8,128)S(1)} %collective-permute-done.25), channel_id=1, source_target_pairs={{0,30},{2,0},{4,2},{6,4},{8,6},{10,8},{12,10},{14,12},{16,14},{18,... | collective-permute-start | bytes 24584 | tf_op jit(solution)/shard_map/ppermute | solution.py:95
  192.1 5.9 %collective-permute-start.27 = (f32[1,64,32]{1,2,0:T(8,128)S(1)}, f32[1,64,32]{1,2,0:T(8,128)S(1)}, u32[]{:S(2)}, u32[]{:S(2)}) collective-permute-start(f32[1,64,32]{1,2,0:T(8,128)S(1)} %collective-permute-done.26), channel_id=1, source_target_pairs={{0,30},{2,0},{4,2},{6,4},{8,6},{10,8},{12,10},{14,12},{16,14},{18,... | collective-permute-start | bytes 24584 | tf_op jit(solution)/shard_map/ppermute | solution.py:95
  198.0 5.9 %collective-permute-start.28 = (f32[1,64,32]{1,2,0:T(8,128)S(1)}, f32[1,64,32]{1,2,0:T(8,128)S(1)}, u32[]{:S(2)}, u32[]{:S(2)}) collective-permute-start(f32[1,64,32]{1,2,0:T(8,128)S(1)} %collective-permute-done.27), channel_id=1, source_target_pairs={{0,30},{2,0},{4,2},{6,4},{8,6},{10,8},{12,10},{14,12},{16,14},{18,... | collective-permute-start | bytes 24584 | tf_op jit(solution)/shard_map/ppermute | solution.py:95
  203.8 5.9 %collective-permute-start.29 = (f32[1,64,32]{1,2,0:T(8,128)S(1)}, f32[1,64,32]{1,2,0:T(8,128)S(1)}, u32[]{:S(2)}, u32[]{:S(2)}) collective-permute-start(f32[1,64,32]{1,2,0:T(8,128)S(1)} %collective-permute-done.28), channel_id=1, source_target_pairs={{0,30},{2,0},{4,2},{6,4},{8,6},{10,8},{12,10},{14,12},{16,14},{18,... | collective-permute-start | bytes 24584 | tf_op jit(solution)/shard_map/ppermute | solution.py:95
  209.7 5.9 %collective-permute-start.30 = (f32[1,64,32]{1,2,0:T(8,128)S(1)}, f32[1,64,32]{1,2,0:T(8,128)S(1)}, u32[]{:S(2)}, u32[]{:S(2)}) collective-permute-start(f32[1,64,32]{1,2,0:T(8,128)S(1)} %collective-permute-done.29), channel_id=1, source_target_pairs={{0,30},{2,0},{4,2},{6,4},{8,6},{10,8},{12,10},{14,12},{16,14},{18,... | collective-permute-start | bytes 24584 | tf_op jit(solution)/shard_map/ppermute | solution.py:95
  215.6 5.9 %collective-permute-start.31 = (f32[1,64,32]{1,2,0:T(8,128)S(1)}, f32[1,64,32]{1,2,0:T(8,128)S(1)}, u32[]{:S(2)}, u32[]{:S(2)}) collective-permute-start(f32[1,64,32]{1,2,0:T(8,128)S(1)} %collective-permute-done.30), channel_id=1, source_target_pairs={{0,30},{2,0},{4,2},{6,4},{8,6},{10,8},{12,10},{14,12},{16,14},{18,... | collective-permute-start | bytes 24584 | tf_op jit(solution)/shard_map/ppermute | solution.py:95
  221.4 5.9 %collective-permute-start.32 = (f32[1,64,32]{1,2,0:T(8,128)S(1)}, f32[1,64,32]{1,2,0:T(8,128)S(1)}, u32[]{:S(2)}, u32[]{:S(2)}) collective-permute-start(f32[1,64,32]{1,2,0:T(8,128)S(1)} %collective-permute-done.31), channel_id=1, source_target_pairs={{0,30},{2,0},{4,2},{6,4},{8,6},{10,8},{12,10},{14,12},{16,14},{18,... | collective-permute-start | bytes 24584 | tf_op jit(solution)/shard_map/ppermute | solution.py:95
  227.3 5.9 %collective-permute-start.33 = (f32[1,64,32]{1,2,0:T(8,128)S(1)}, f32[1,64,32]{1,2,0:T(8,128)S(1)}, u32[]{:S(2)}, u32[]{:S(2)}) collective-permute-start(f32[1,64,32]{1,2,0:T(8,128)S(1)} %collective-permute-done.32), channel_id=1, source_target_pairs={{0,30},{2,0},{4,2},{6,4},{8,6},{10,8},{12,10},{14,12},{16,14},{18,... | collective-permute-start | bytes 24584 | tf_op jit(solution)/shard_map/ppermute | solution.py:95
  233.1 5.9 %collective-permute-start.34 = (f32[1,64,32]{1,2,0:T(8,128)S(1)}, f32[1,64,32]{1,2,0:T(8,128)S(1)}, u32[]{:S(2)}, u32[]{:S(2)}) collective-permute-start(f32[1,64,32]{1,2,0:T(8,128)S(1)} %collective-permute-done.33), channel_id=1, source_target_pairs={{0,30},{2,0},{4,2},{6,4},{8,6},{10,8},{12,10},{14,12},{16,14},{18,... | collective-permute-start | bytes 24584 | tf_op jit(solution)/shard_map/ppermute | solution.py:95
  239.0 5.9 %collective-permute-start.35 = (f32[1,64,32]{1,2,0:T(8,128)S(1)}, f32[1,64,32]{1,2,0:T(8,128)S(1)}, u32[]{:S(2)}, u32[]{:S(2)}) collective-permute-start(f32[1,64,32]{1,2,0:T(8,128)S(1)} %collective-permute-done.34), channel_id=1, source_target_pairs={{0,30},{2,0},{4,2},{6,4},{8,6},{10,8},{12,10},{14,12},{16,14},{18,... | collective-permute-start | bytes 24584 | tf_op jit(solution)/shard_map/ppermute | solution.py:95
  244.9 5.9 %collective-permute-start.36 = (f32[1,64,32]{1,2,0:T(8,128)S(1)}, f32[1,64,32]{1,2,0:T(8,128)S(1)}, u32[]{:S(2)}, u32[]{:S(2)}) collective-permute-start(f32[1,64,32]{1,2,0:T(8,128)S(1)} %collective-permute-done.35), channel_id=1, source_target_pairs={{0,30},{2,0},{4,2},{6,4},{8,6},{10,8},{12,10},{14,12},{16,14},{18,... | collective-permute-start | bytes 24584 | tf_op jit(solution)/shard_map/ppermute | solution.py:95
  250.7 5.9 %collective-permute-start.37 = (f32[1,64,32]{1,2,0:T(8,128)S(1)}, f32[1,64,32]{1,2,0:T(8,128)S(1)}, u32[]{:S(2)}, u32[]{:S(2)}) collective-permute-start(f32[1,64,32]{1,2,0:T(8,128)S(1)} %collective-permute-done.36), channel_id=1, source_target_pairs={{0,30},{2,0},{4,2},{6,4},{8,6},{10,8},{12,10},{14,12},{16,14},{18,... | collective-permute-start | bytes 24584 | tf_op jit(solution)/shard_map/ppermute | solution.py:95
